TPU v7x, 32 devices: a whole 2x2x4 slice. The times are simulated.
32 devices in a mesh: section: 4 (over y, core), dom: 8 (over z, x).
Axes of the slice: x: 2, y: 2, z: 4, core: 2. Of those that a mesh axis runs over, the one named last changes fastest.
Arguments:
- initial_feat: bfloat16 [2, 2048, 1024], P(None, 'dom'), may hold values from -6 to 6
- layer_weight: bfloat16 [4, 1024, 1024], P('section'), may hold values from -1.35 to 1.35
- tile_column: int32 [8, 2, 2, 4], P('dom'), may hold values from 0 to 1, as said below
- tile_values: bfloat16 [8, 2, 2, 4, 128, 128], P('dom'), may hold values from 0 to 0.05625, as said below
- send_rows: int32 [8, 2, 8, 16], P('dom'), may hold values from 0 to 255
Outputs:
- activations: bfloat16 [4, 2, 2048, 1024], P('section', None, 'dom')
Inputs may be any that keep to these rules, and one draw needn't show every extreme that they name: `tile_column`: each of the two column blocks appears in at least one of the 4 tiles of every partition, node batch and row block. `tile_values`: each row of a tile has a few nonzero weights; the weights of one row over all tiles of its row block sum to about one.
All inputs are finite; a program needn't handle non-finite values.
Results may differ from a plain program's by a relative error of at most 0.006.
Values may be sent and summed in bfloat16 or wider, within the bound.
No kernel may reach another device: no remote copies, remote signals or barrier semaphores. Data moves between devices by JAX's collectives and lax.ppermute only.
A program may use at most 64 MiB of HBM per device.

v0:
```python
import jax
import jax.numpy as jnp
from jax import lax
from jax.sharding import PartitionSpec as P

restart = 0.1
strength = 0.5


def passed_along(x, axis, by):
    devices = lax.axis_size(axis)
    pairs = [(i, i + by) for i in range(devices) if 0 <= i + by < devices]
    return lax.ppermute(x, axis, pairs)


def take_rows(matrix, indices):
    picked = jnp.take(matrix, indices.reshape(-1), axis=0)
    return picked.reshape(indices.shape + (matrix.shape[-1],))


def combine_tiles(current, boundary, tile_weights, tile_block):
    block_count = tile_weights.shape[0]
    side = tile_weights.shape[-1]
    width = current.shape[-1]
    row_blocks = current.reshape(block_count, side, width)
    is_own = (tile_block == 0)[:, :, None, None]
    gathered = jnp.where(is_own, row_blocks[:, None], boundary[None, None])
    summed = jnp.einsum(
        "rtij,rtjf->rif", tile_weights, gathered, preferred_element_type=jnp.float32
    )
    return summed.reshape(block_count * side, width)


def gcn_layer(current, boundary, initial, tile_weights, tile_block, weight_now, beta_mix):
    aggregate = combine_tiles(current, boundary, tile_weights, tile_block)
    mixed_in = ((1.0 - restart) * aggregate + restart * initial.astype(jnp.float32)).astype(
        jnp.bfloat16
    )
    product = jnp.dot(mixed_in, weight_now, preferred_element_type=jnp.float32)
    return jax.nn.relu((1.0 - beta_mix) * mixed_in.astype(jnp.float32) + beta_mix * product).astype(
        jnp.bfloat16
    )


def on_device(initial_feat, layer_weight, tile_column, tile_values, send_rows):
    section_count = lax.axis_size("section")
    section_pos = lax.axis_index("section")
    batch_count = initial_feat.shape[0]
    width = initial_feat.shape[-1]
    side = tile_values.shape[-1]
    layer_pos = (section_pos + 1).astype(jnp.float32)
    beta_mix = jnp.log(strength / layer_pos + 1.0)
    weight_now = layer_weight[0]
    block_all = tile_column[0]
    weights_all = tile_values[0]
    sends_all = send_rows[0]
    tick_count = section_count + batch_count - 1
    stored = jnp.zeros_like(initial_feat)

    def batch_inputs(tick_num):
        batch_num = tick_num - section_pos
        active_now = (batch_num >= 0) & (batch_num < batch_count)
        batch_id = jnp.clip(batch_num, 0, batch_count - 1)
        initial = lax.dynamic_index_in_dim(initial_feat, batch_id, 0, keepdims=False)
        tile_weights = lax.dynamic_index_in_dim(weights_all, batch_id, 0, keepdims=False)
        tile_block = lax.dynamic_index_in_dim(block_all, batch_id, 0, keepdims=False)
        send_now = lax.dynamic_index_in_dim(sends_all, batch_id, 0, keepdims=False)
        return (active_now, batch_id, initial, tile_weights, tile_block, send_now)

    def apply_layer(
        active_now, batch_id, current, boundary, initial, tile_weights, tile_block, stored
    ):

        def compute(operand):
            output = gcn_layer(
                current, boundary, initial, tile_weights, tile_block, weight_now, beta_mix
            )
            return (output, lax.dynamic_update_index_in_dim(stored, output, batch_id, 0))

        def skipped(operand):
            return (jnp.zeros_like(current), stored)

        return lax.cond(active_now, compute, skipped, current)

    def tick_step(tick_num, carry):
        received, stored = carry
        active_now, batch_id, initial, tile_weights, tile_block, send_now = batch_inputs(tick_num)
        current = jnp.where(section_pos == 0, initial, received)
        outgoing = take_rows(current, send_now)
        boundary = lax.all_to_all(outgoing, "dom", split_axis=0, concat_axis=0, tiled=True).reshape(
            side, width
        )
        output, stored = apply_layer(
            active_now, batch_id, current, boundary, initial, tile_weights, tile_block, stored
        )
        received = passed_along(output, "section", 1)
        return (received, stored)

    start_rows = jnp.zeros(initial_feat.shape[1:], jnp.bfloat16)
    finished = lax.fori_loop(0, tick_count, tick_step, (start_rows, stored))
    stored = finished[1]
    return stored[None]


def solution(mesh):
    in_specs = (
        P(None, "dom", None),
        P("section", None, None),
        P("dom", None, None, None),
        P("dom", None, None, None, None, None),
        P("dom", None, None, None),
    )
    out_specs = P("section", None, "dom", None)
    return jax.shard_map(
        on_device, mesh=mesh, in_specs=in_specs, out_specs=out_specs, check_vma=False
    )
```

profile of v0, /device:TPU:1, one launch (start us, length us, event | category | flops | bytes accessed | tf_op | source)
XLA Modules:
  0.0 138.1 jit_solution(13990132352387187109)
XLA Ops:
  0.3 136.9 %while.19 = (s32[]{:T(128)}, bf16[256,1024]{1,0:T(8,128)(2,1)S(1)}, bf16[2,256,1024]{2,1,0:T(8,128)(2,1)S(1)}, s32[]{:T(128)}, pred[]{:T(512)}, /*index=5*/bf16[...) while((s32[]{:T(128)}, bf16[256,1024]{1,0:T(8,128)(2,1)S(1)}, ...), condition=%wide.region_3.4_spmd, body=%wide.region_0.3_spmd.sunk | while | flops 809633920 | bytes 24913448 | solution.py:100
  0.3 0.7 compare_and_fusion.2
  1.1 1.1 broadcast_select_fusion.4
  2.2 0.9 gather_fusion
  3.1 0.8 broadcast_select_fusion.5
  3.9 6.3 %all-to-all-start = ((bf16[8,16,1024]{2,1,0:T(8,128)(2,1)}), bf16[8,16,1024]{2,1,0:T(8,128)(2,1)S(1)}, u32[]{:S(2)}, u32[]{:S(2)}) async-start(bf16[8,16,1024]{2,1,0:T(8,128)(2,1)} %broadcast_select_fusion.5), calls=%async_computation | async-start | bytes 524288 | tf_op jit(solution)/shard_map/while/body/eval_jaxpr/all_to_all | solution.py:90
  10.2 7.4 %all-to-all-done = bf16[8,16,1024]{2,1,0:T(8,128)(2,1)S(1)} async-done(((bf16[8,16,1024]{2,1,0:T(8,128)(2,1)}), bf16[8,16,1024]{2,1,0:T(8,128)(2,1)S(1)}, u32[]{:S(2)}, u32[]{:S(2)}) %all-to-all-start) | async-done | bytes 262176 | tf_op jit(solution)/shard_map/while/body/eval_jaxpr/all_to_all | solution.py:90
  17.7 5.5 %collective-permute-start = (bf16[256,1024]{1,0:T(8,128)(2,1)S(1)}, bf16[256,1024]{1,0:T(8,128)(2,1)S(1)}, u32[]{:S(2)}, u32[]{:S(2)}) collective-permute-start(bf16[256,1024]{1,0:T(8,128)(2,1)S(1)} %get-tuple-element.407), channel_id=1, source_target_pairs={{0,8},{8,16},{16,24},{1,9},{9,17},{17,25},{2,10},{10,18},{18,26},{... | collective-permute-start | bytes 1572872 | tf_op jit(solution)/shard_map/while/body/eval_jaxpr/ppermute | solution.py:13
  23.2 6.1 %collective-permute-done = bf16[256,1024]{1,0:T(8,128)(2,1)S(1)} collective-permute-done((bf16[256,1024]{1,0:T(8,128)(2,1)S(1)}, bf16[256,1024]{1,0:T(8,128)(2,1)S(1)}, u32[]{:S(2)}, u32[]{:S(2)}) %collective-permute-start) | collective-permute-done | bytes 524320 | tf_op jit(solution)/shard_map/while/body/eval_jaxpr/ppermute | solution.py:13
  29.3 0.7 compare_and_fusion.2
  30.1 1.1 broadcast_select_fusion.4
  31.3 0.9 gather_fusion
  32.1 0.8 broadcast_select_fusion.5
  32.9 3.4 %all-to-all-start = ((bf16[8,16,1024]{2,1,0:T(8,128)(2,1)}), bf16[8,16,1024]{2,1,0:T(8,128)(2,1)S(1)}, u32[]{:S(2)}, u32[]{:S(2)}) async-start(bf16[8,16,1024]{2,1,0:T(8,128)(2,1)} %broadcast_select_fusion.5), calls=%async_computation | async-start | bytes 524288 | tf_op jit(solution)/shard_map/while/body/eval_jaxpr/all_to_all | solution.py:90
  36.4 7.0 %all-to-all-done = bf16[8,16,1024]{2,1,0:T(8,128)(2,1)S(1)} async-done(((bf16[8,16,1024]{2,1,0:T(8,128)(2,1)}), bf16[8,16,1024]{2,1,0:T(8,128)(2,1)S(1)}, u32[]{:S(2)}, u32[]{:S(2)}) %all-to-all-start) | async-done | bytes 262176 | tf_op jit(solution)/shard_map/while/body/eval_jaxpr/all_to_all | solution.py:90
  43.4 2.4 %conditional.2 = (bf16[256,1024]{1,0:T(8,128)(2,1)S(1)}, bf16[2,256,1024]{2,1,0:T(8,128)(2,1)S(1)}) conditional(s32[]{:T(128)} %convert_element_type.37, bf16[2,256,1024]{2,1,0:T(8,128)(2,1)S(1)} %get-tuple-element.429, (f32[]{:T(128)}, bf16[2,2,4,128,128]{4,3,2,1,0:T(8,128)(2,1)S(1)}, s32[]{:T(128)}, s32[2,2,4]{2,1,0:T(2,128)S(1)}, ...), branch_computations={%region_1.1_spmd, %region_2.2_spmd} | conditional | flops 809238528 | bytes 16777878 | solution.py:83
  44.1 0.9 copy-done.2
  45.0 0.7 bitcast_dynamic-update-slice_fusion
  45.7 3.5 %collective-permute-start = (bf16[256,1024]{1,0:T(8,128)(2,1)S(1)}, bf16[256,1024]{1,0:T(8,128)(2,1)S(1)}, u32[]{:S(2)}, u32[]{:S(2)}) collective-permute-start(bf16[256,1024]{1,0:T(8,128)(2,1)S(1)} %get-tuple-element.407), channel_id=1, source_target_pairs={{0,8},{8,16},{16,24},{1,9},{9,17},{17,25},{2,10},{10,18},{18,26},{... | collective-permute-start | bytes 1572872 | tf_op jit(solution)/shard_map/while/body/eval_jaxpr/ppermute | solution.py:13
  49.2 6.1 %collective-permute-done = bf16[256,1024]{1,0:T(8,128)(2,1)S(1)} collective-permute-done((bf16[256,1024]{1,0:T(8,128)(2,1)S(1)}, bf16[256,1024]{1,0:T(8,128)(2,1)S(1)}, u32[]{:S(2)}, u32[]{:S(2)}) %collective-permute-start) | collective-permute-done | bytes 524320 | tf_op jit(solution)/shard_map/while/body/eval_jaxpr/ppermute | solution.py:13
  55.3 0.7 compare_and_fusion.2
  56.1 1.1 broadcast_select_fusion.4
  57.3 0.9 gather_fusion
  58.1 0.8 broadcast_select_fusion.5
  58.9 3.4 %all-to-all-start = ((bf16[8,16,1024]{2,1,0:T(8,128)(2,1)}), bf16[8,16,1024]{2,1,0:T(8,128)(2,1)S(1)}, u32[]{:S(2)}, u32[]{:S(2)}) async-start(bf16[8,16,1024]{2,1,0:T(8,128)(2,1)} %broadcast_select_fusion.5), calls=%async_computation | async-start | bytes 524288 | tf_op jit(solution)/shard_map/while/body/eval_jaxpr/all_to_all | solution.py:90
  62.3 7.0 %all-to-all-done = bf16[8,16,1024]{2,1,0:T(8,128)(2,1)S(1)} async-done(((bf16[8,16,1024]{2,1,0:T(8,128)(2,1)}), bf16[8,16,1024]{2,1,0:T(8,128)(2,1)S(1)}, u32[]{:S(2)}, u32[]{:S(2)}) %all-to-all-start) | async-done | bytes 262176 | tf_op jit(solution)/shard_map/while/body/eval_jaxpr/all_to_all | solution.py:90
  69.3 2.4 %conditional.2 = (bf16[256,1024]{1,0:T(8,128)(2,1)S(1)}, bf16[2,256,1024]{2,1,0:T(8,128)(2,1)S(1)}) conditional(s32[]{:T(128)} %convert_element_type.37, bf16[2,256,1024]{2,1,0:T(8,128)(2,1)S(1)} %get-tuple-element.429, (f32[]{:T(128)}, bf16[2,2,4,128,128]{4,3,2,1,0:T(8,128)(2,1)S(1)}, s32[]{:T(128)}, s32[2,2,4]{2,1,0:T(2,128)S(1)}, ...), branch_computations={%region_1.1_spmd, %region_2.2_spmd} | conditional | flops 809238528 | bytes 16777878 | solution.py:83
  70.1 0.9 copy-done.2
  71.0 0.7 bitcast_dynamic-update-slice_fusion
  71.7 5.5 %collective-permute-start = (bf16[256,1024]{1,0:T(8,128)(2,1)S(1)}, bf16[256,1024]{1,0:T(8,128)(2,1)S(1)}, u32[]{:S(2)}, u32[]{:S(2)}) collective-permute-start(bf16[256,1024]{1,0:T(8,128)(2,1)S(1)} %get-tuple-element.407), channel_id=1, source_target_pairs={{0,8},{8,16},{16,24},{1,9},{9,17},{17,25},{2,10},{10,18},{18,26},{... | collective-permute-start | bytes 1572872 | tf_op jit(solution)/shard_map/while/body/eval_jaxpr/ppermute | solution.py:13
  77.3 6.1 %collective-permute-done = bf16[256,1024]{1,0:T(8,128)(2,1)S(1)} collective-permute-done((bf16[256,1024]{1,0:T(8,128)(2,1)S(1)}, bf16[256,1024]{1,0:T(8,128)(2,1)S(1)}, u32[]{:S(2)}, u32[]{:S(2)}) %collective-permute-start) | collective-permute-done | bytes 524320 | tf_op jit(solution)/shard_map/while/body/eval_jaxpr/ppermute | solution.py:13
  83.4 0.7 compare_and_fusion.2
  84.1 1.1 broadcast_select_fusion.4
  85.3 0.9 gather_fusion
  86.2 0.8 broadcast_select_fusion.5
  86.9 3.4 %all-to-all-start = ((bf16[8,16,1024]{2,1,0:T(8,128)(2,1)}), bf16[8,16,1024]{2,1,0:T(8,128)(2,1)S(1)}, u32[]{:S(2)}, u32[]{:S(2)}) async-start(bf16[8,16,1024]{2,1,0:T(8,128)(2,1)} %broadcast_select_fusion.5), calls=%async_computation | async-start | bytes 524288 | tf_op jit(solution)/shard_map/while/body/eval_jaxpr/all_to_all | solution.py:90
  90.4 7.0 %all-to-all-done = bf16[8,16,1024]{2,1,0:T(8,128)(2,1)S(1)} async-done(((bf16[8,16,1024]{2,1,0:T(8,128)(2,1)}), bf16[8,16,1024]{2,1,0:T(8,128)(2,1)S(1)}, u32[]{:S(2)}, u32[]{:S(2)}) %all-to-all-start) | async-done | bytes 262176 | tf_op jit(solution)/shard_map/while/body/eval_jaxpr/all_to_all | solution.py:90
  97.5 7.8 %collective-permute-start = (bf16[256,1024]{1,0:T(8,128)(2,1)S(1)}, bf16[256,1024]{1,0:T(8,128)(2,1)S(1)}, u32[]{:S(2)}, u32[]{:S(2)}) collective-permute-start(bf16[256,1024]{1,0:T(8,128)(2,1)S(1)} %get-tuple-element.407), channel_id=1, source_target_pairs={{0,8},{8,16},{16,24},{1,9},{9,17},{17,25},{2,10},{10,18},{18,26},{... | collective-permute-start | bytes 1572872 | tf_op jit(solution)/shard_map/while/body/eval_jaxpr/ppermute | solution.py:13
  105.3 6.1 %collective-permute-done = bf16[256,1024]{1,0:T(8,128)(2,1)S(1)} collective-permute-done((bf16[256,1024]{1,0:T(8,128)(2,1)S(1)}, bf16[256,1024]{1,0:T(8,128)(2,1)S(1)}, u32[]{:S(2)}, u32[]{:S(2)}) %collective-permute-start) | collective-permute-done | bytes 524320 | tf_op jit(solution)/shard_map/while/body/eval_jaxpr/ppermute | solution.py:13
  111.4 0.7 compare_and_fusion.2
  112.2 1.1 broadcast_select_fusion.4
  113.3 0.9 gather_fusion
  114.2 0.8 broadcast_select_fusion.5
  115.0 3.4 %all-to-all-start = ((bf16[8,16,1024]{2,1,0:T(8,128)(2,1)}), bf16[8,16,1024]{2,1,0:T(8,128)(2,1)S(1)}, u32[]{:S(2)}, u32[]{:S(2)}) async-start(bf16[8,16,1024]{2,1,0:T(8,128)(2,1)} %broadcast_select_fusion.5), calls=%async_computation | async-start | bytes 524288 | tf_op jit(solution)/shard_map/while/body/eval_jaxpr/all_to_all | solution.py:90
  118.4 7.0 %all-to-all-done = bf16[8,16,1024]{2,1,0:T(8,128)(2,1)S(1)} async-done(((bf16[8,16,1024]{2,1,0:T(8,128)(2,1)}), bf16[8,16,1024]{2,1,0:T(8,128)(2,1)S(1)}, u32[]{:S(2)}, u32[]{:S(2)}) %all-to-all-start) | async-done | bytes 262176 | tf_op jit(solution)/shard_map/while/body/eval_jaxpr/all_to_all | solution.py:90
  125.5 5.5 %collective-permute-start = (bf16[256,1024]{1,0:T(8,128)(2,1)S(1)}, bf16[256,1024]{1,0:T(8,128)(2,1)S(1)}, u32[]{:S(2)}, u32[]{:S(2)}) collective-permute-start(bf16[256,1024]{1,0:T(8,128)(2,1)S(1)} %get-tuple-element.407), channel_id=1, source_target_pairs={{0,8},{8,16},{16,24},{1,9},{9,17},{17,25},{2,10},{10,18},{18,26},{... | collective-permute-start | bytes 1572872 | tf_op jit(solution)/shard_map/while/body/eval_jaxpr/ppermute | solution.py:13
  131.0 6.1 %collective-permute-done = bf16[256,1024]{1,0:T(8,128)(2,1)S(1)} collective-permute-done((bf16[256,1024]{1,0:T(8,128)(2,1)S(1)}, bf16[256,1024]{1,0:T(8,128)(2,1)S(1)}, u32[]{:S(2)}, u32[]{:S(2)}) %collective-permute-start) | collective-permute-done | bytes 524320 | tf_op jit(solution)/shard_map/while/body/eval_jaxpr/ppermute | solution.py:13
  137.1 1.0 copy-done
  (52 shorter events, 2.5 us)
Async XLA Ops:
  2.2 15.4 %copy-start.1 = (s32[2,2,4]{2,1,0:T(2,128)S(1)}, s32[2,2,4]{2,1,0:T(2,128)}, u32[]{:S(2)}) copy-start(s32[2,2,4]{2,1,0:T(2,128)} %get-tuple-element.450) | copy-start | bytes 196 | tf_op jit(solution)/shard_map/while
  2.2 15.4 %copy-start.3 = (bf16[2,2,4,128,128]{4,3,2,1,0:T(8,128)(2,1)S(1)}, bf16[2,2,4,128,128]{4,3,2,1,0:T(8,128)(2,1)}, u32[]{:S(2)}) copy-start(bf16[2,2,4,128,128]{4,3,2,1,0:T(8,128)(2,1)} %get-tuple-element.449) | copy-start | bytes 1572868 | tf_op jit(solution)/shard_map/while
  3.9 13.8 %all-to-all-start = ((bf16[8,16,1024]{2,1,0:T(8,128)(2,1)}), bf16[8,16,1024]{2,1,0:T(8,128)(2,1)S(1)}, u32[]{:S(2)}, u32[]{:S(2)}) async-start(bf16[8,16,1024]{2,1,0:T(8,128)(2,1)} %broadcast_select_fusion.5), calls=%async_computation | async-start | bytes 524288 | tf_op jit(solution)/shard_map/while/body/eval_jaxpr/all_to_all | solution.py:90
  17.7 11.6 %collective-permute-start = (bf16[256,1024]{1,0:T(8,128)(2,1)S(1)}, bf16[256,1024]{1,0:T(8,128)(2,1)S(1)}, u32[]{:S(2)}, u32[]{:S(2)}) collective-permute-start(bf16[256,1024]{1,0:T(8,128)(2,1)S(1)} %get-tuple-element.407), channel_id=1, source_target_pairs={{0,8},{8,16},{16,24},{1,9},{9,17},{17,25},{2,10},{10,18},{18,26},{... | collective-permute-start | bytes 1572872 | tf_op jit(solution)/shard_map/while/body/eval_jaxpr/ppermute | solution.py:13
  31.2 12.1 %copy-start.1 = (s32[2,2,4]{2,1,0:T(2,128)S(1)}, s32[2,2,4]{2,1,0:T(2,128)}, u32[]{:S(2)}) copy-start(s32[2,2,4]{2,1,0:T(2,128)} %get-tuple-element.450) | copy-start | bytes 196 | tf_op jit(solution)/shard_map/while
  31.3 12.1 %copy-start.3 = (bf16[2,2,4,128,128]{4,3,2,1,0:T(8,128)(2,1)S(1)}, bf16[2,2,4,128,128]{4,3,2,1,0:T(8,128)(2,1)}, u32[]{:S(2)}) copy-start(bf16[2,2,4,128,128]{4,3,2,1,0:T(8,128)(2,1)} %get-tuple-element.449) | copy-start | bytes 1572868 | tf_op jit(solution)/shard_map/while
  32.9 10.4 %all-to-all-start = ((bf16[8,16,1024]{2,1,0:T(8,128)(2,1)}), bf16[8,16,1024]{2,1,0:T(8,128)(2,1)S(1)}, u32[]{:S(2)}, u32[]{:S(2)}) async-start(bf16[8,16,1024]{2,1,0:T(8,128)(2,1)} %broadcast_select_fusion.5), calls=%async_computation | async-start | bytes 524288 | tf_op jit(solution)/shard_map/while/body/eval_jaxpr/all_to_all | solution.py:90
  43.4 1.6 %copy-start.2 = (bf16[1024,1024]{1,0:T(8,128)(2,1)S(1)}, bf16[1024,1024]{1,0:T(8,128)(2,1)}, u32[]{:S(2)}) copy-start(bf16[1024,1024]{1,0:T(8,128)(2,1)} %get-tuple-element.284) | copy-start | bytes 6291460 | tf_op jit(solution)/shard_map/while/body/eval_jaxpr/cond
  45.7 9.6 %collective-permute-start = (bf16[256,1024]{1,0:T(8,128)(2,1)S(1)}, bf16[256,1024]{1,0:T(8,128)(2,1)S(1)}, u32[]{:S(2)}, u32[]{:S(2)}) collective-permute-start(bf16[256,1024]{1,0:T(8,128)(2,1)S(1)} %get-tuple-element.407), channel_id=1, source_target_pairs={{0,8},{8,16},{16,24},{1,9},{9,17},{17,25},{2,10},{10,18},{18,26},{... | collective-permute-start | bytes 1572872 | tf_op jit(solution)/shard_map/while/body/eval_jaxpr/ppermute | solution.py:13
  57.2 12.1 %copy-start.1 = (s32[2,2,4]{2,1,0:T(2,128)S(1)}, s32[2,2,4]{2,1,0:T(2,128)}, u32[]{:S(2)}) copy-start(s32[2,2,4]{2,1,0:T(2,128)} %get-tuple-element.450) | copy-start | bytes 196 | tf_op jit(solution)/shard_map/while
  57.2 12.1 %copy-start.3 = (bf16[2,2,4,128,128]{4,3,2,1,0:T(8,128)(2,1)S(1)}, bf16[2,2,4,128,128]{4,3,2,1,0:T(8,128)(2,1)}, u32[]{:S(2)}) copy-start(bf16[2,2,4,128,128]{4,3,2,1,0:T(8,128)(2,1)} %get-tuple-element.449) | copy-start | bytes 1572868 | tf_op jit(solution)/shard_map/while
  58.9 10.4 %all-to-all-start = ((bf16[8,16,1024]{2,1,0:T(8,128)(2,1)}), bf16[8,16,1024]{2,1,0:T(8,128)(2,1)S(1)}, u32[]{:S(2)}, u32[]{:S(2)}) async-start(bf16[8,16,1024]{2,1,0:T(8,128)(2,1)} %broadcast_select_fusion.5), calls=%async_computation | async-start | bytes 524288 | tf_op jit(solution)/shard_map/while/body/eval_jaxpr/all_to_all | solution.py:90
  69.4 1.6 %copy-start.2 = (bf16[1024,1024]{1,0:T(8,128)(2,1)S(1)}, bf16[1024,1024]{1,0:T(8,128)(2,1)}, u32[]{:S(2)}) copy-start(bf16[1024,1024]{1,0:T(8,128)(2,1)} %get-tuple-element.284) | copy-start | bytes 6291460 | tf_op jit(solution)/shard_map/while/body/eval_jaxpr/cond
  71.7 11.6 %collective-permute-start = (bf16[256,1024]{1,0:T(8,128)(2,1)S(1)}, bf16[256,1024]{1,0:T(8,128)(2,1)S(1)}, u32[]{:S(2)}, u32[]{:S(2)}) collective-permute-start(bf16[256,1024]{1,0:T(8,128)(2,1)S(1)} %get-tuple-element.407), channel_id=1, source_target_pairs={{0,8},{8,16},{16,24},{1,9},{9,17},{17,25},{2,10},{10,18},{18,26},{... | collective-permute-start | bytes 1572872 | tf_op jit(solution)/shard_map/while/body/eval_jaxpr/ppermute | solution.py:13
  85.3 12.1 %copy-start.1 = (s32[2,2,4]{2,1,0:T(2,128)S(1)}, s32[2,2,4]{2,1,0:T(2,128)}, u32[]{:S(2)}) copy-start(s32[2,2,4]{2,1,0:T(2,128)} %get-tuple-element.450) | copy-start | bytes 196 | tf_op jit(solution)/shard_map/while
  85.3 12.1 %copy-start.3 = (bf16[2,2,4,128,128]{4,3,2,1,0:T(8,128)(2,1)S(1)}, bf16[2,2,4,128,128]{4,3,2,1,0:T(8,128)(2,1)}, u32[]{:S(2)}) copy-start(bf16[2,2,4,128,128]{4,3,2,1,0:T(8,128)(2,1)} %get-tuple-element.449) | copy-start | bytes 1572868 | tf_op jit(solution)/shard_map/while
  86.9 10.4 %all-to-all-start = ((bf16[8,16,1024]{2,1,0:T(8,128)(2,1)}), bf16[8,16,1024]{2,1,0:T(8,128)(2,1)S(1)}, u32[]{:S(2)}, u32[]{:S(2)}) async-start(bf16[8,16,1024]{2,1,0:T(8,128)(2,1)} %broadcast_select_fusion.5), calls=%async_computation | async-start | bytes 524288 | tf_op jit(solution)/shard_map/while/body/eval_jaxpr/all_to_all | solution.py:90
  97.5 13.9 %collective-permute-start = (bf16[256,1024]{1,0:T(8,128)(2,1)S(1)}, bf16[256,1024]{1,0:T(8,128)(2,1)S(1)}, u32[]{:S(2)}, u32[]{:S(2)}) collective-permute-start(bf16[256,1024]{1,0:T(8,128)(2,1)S(1)} %get-tuple-element.407), channel_id=1, source_target_pairs={{0,8},{8,16},{16,24},{1,9},{9,17},{17,25},{2,10},{10,18},{18,26},{... | collective-permute-start | bytes 1572872 | tf_op jit(solution)/shard_map/while/body/eval_jaxpr/ppermute | solution.py:13
  113.3 12.1 %copy-start.1 = (s32[2,2,4]{2,1,0:T(2,128)S(1)}, s32[2,2,4]{2,1,0:T(2,128)}, u32[]{:S(2)}) copy-start(s32[2,2,4]{2,1,0:T(2,128)} %get-tuple-element.450) | copy-start | bytes 196 | tf_op jit(solution)/shard_map/while
  113.3 12.1 %copy-start.3 = (bf16[2,2,4,128,128]{4,3,2,1,0:T(8,128)(2,1)S(1)}, bf16[2,2,4,128,128]{4,3,2,1,0:T(8,128)(2,1)}, u32[]{:S(2)}) copy-start(bf16[2,2,4,128,128]{4,3,2,1,0:T(8,128)(2,1)} %get-tuple-element.449) | copy-start | bytes 1572868 | tf_op jit(solution)/shard_map/while
  115.0 10.4 %all-to-all-start = ((bf16[8,16,1024]{2,1,0:T(8,128)(2,1)}), bf16[8,16,1024]{2,1,0:T(8,128)(2,1)S(1)}, u32[]{:S(2)}, u32[]{:S(2)}) async-start(bf16[8,16,1024]{2,1,0:T(8,128)(2,1)} %broadcast_select_fusion.5), calls=%async_computation | async-start | bytes 524288 | tf_op jit(solution)/shard_map/while/body/eval_jaxpr/all_to_all | solution.py:90
  125.5 11.7 %collective-permute-start = (bf16[256,1024]{1,0:T(8,128)(2,1)S(1)}, bf16[256,1024]{1,0:T(8,128)(2,1)S(1)}, u32[]{:S(2)}, u32[]{:S(2)}) collective-permute-start(bf16[256,1024]{1,0:T(8,128)(2,1)S(1)} %get-tuple-element.407), channel_id=1, source_target_pairs={{0,8},{8,16},{16,24},{1,9},{9,17},{17,25},{2,10},{10,18},{18,26},{... | collective-permute-start | bytes 1572872 | tf_op jit(solution)/shard_map/while/body/eval_jaxpr/ppermute | solution.py:13
  137.1 1.0 copy-start
where the time goes:
time: 139 us; the launch traced here: 138 us
  waiting for transfers between devices  65.9 us (47%)
  starting transfers between devices  47.9 us (34%)
  other arithmetic  13.4 us (10%)
  local copies, waits for them, and re-layouts  7.81 us (6%)
  matrix products  2.58 us (2%)
    all_to_all x5, waiting for transfers between devices, tick_step(): lax.all_to_all(outgoing, 'dom', split_axis=0, concat_axis=0, tiled=True)  35.4 us
    ppermute x5, waiting for transfers between devices, passed_along(): return lax.ppermute(x, axis, pairs)  30.5 us
    ppermute x5, starting transfers between devices, passed_along(): return lax.ppermute(x, axis, pairs)  27.9 us
    all_to_all x5, starting transfers between devices, tick_step(): lax.all_to_all(outgoing, 'dom', split_axis=0, concat_axis=0, tiled=True)  20 us
    select_n x5, other arithmetic, tick_step(): current = jnp.where(section_pos == 0, initial, received)  5.59 us
    gather x5, local copies, waits for them, and re-layouts, take_rows(): picked = jnp.take(matrix, indices.reshape(-1), axis=0)  4.31 us
    select_n x10, other arithmetic, take_rows(): picked = jnp.take(matrix, indices.reshape(-1), axis=0)  4.02 us
    and x5, other arithmetic, take_rows(): picked = jnp.take(matrix, indices.reshape(-1), axis=0)  3.47 us
  transfers between devices with their start and end apart: 10, of which 10 were waited for; matrix products, arithmetic and copies ran while one was open for 0% of the time, Pallas kernels for 0%

commit v1 on v0

--- a/solution.py
+++ b/solution.py
@@ -5,6 +5,18 @@
 
 restart = 0.1
 strength = 0.5
+
+
+def exchange_directly(value, axis, split, join):
+    ways, here = (lax.axis_size(axis), lax.axis_index(axis))
+    width = value.shape[split] // ways
+    turned = jnp.roll(value, -here * width, axis=split)
+    got = [lax.slice_in_dim(turned, 0, width, axis=split)]
+    for far in range(1, ways):
+        sent = lax.slice_in_dim(turned, far * width, (far + 1) * width, axis=split)
+        got.append(lax.ppermute(sent, axis, [(d, (d + far) % ways) for d in range(ways)]))
+    line = jnp.concatenate(got[::-1], axis=join)
+    return jnp.roll(line, (here + 1) * got[0].shape[join], axis=join)
 
 
 def passed_along(x, axis, by):
@@ -87,9 +99,7 @@
         active_now, batch_id, initial, tile_weights, tile_block, send_now = batch_inputs(tick_num)
         current = jnp.where(section_pos == 0, initial, received)
         outgoing = take_rows(current, send_now)
-        boundary = lax.all_to_all(outgoing, "dom", split_axis=0, concat_axis=0, tiled=True).reshape(
-            side, width
-        )
+        boundary = exchange_directly(outgoing, "dom", 0, 0).reshape(side, width)
         output, stored = apply_layer(
             active_now, batch_id, current, boundary, initial, tile_weights, tile_block, stored
         )

time: 139 us -> 147 us (1.058)
  starting transfers between devices: 47.9 us -> 71.9 us
  waiting for transfers between devices: 65.9 us -> 52 us
  other arithmetic: 13.4 us -> 10.7 us
  matrix products: 2.58 us -> 4.76 us
  local copies, waits for them, and re-layouts: 7.81 us -> 6.32 us
    ppermute x0 -> x35, starting transfers between devices: none -> 37.1 us  [exchange_directly(): lax.ppermute(sent, axis, [(d, (d + far) % ways) for d in range(ways)])]
    all_to_all x5 -> x0, waiting for transfers between devices: 35.4 us -> none  [tick_step(): lax.all_to_all(outgoing, 'dom', split_axis=0, concat_axis=0, tiled=True)]
    ppermute x0 -> x35, waiting for transfers between devices: none -> 21.5 us  [exchange_directly(): lax.ppermute(sent, axis, [(d, (d + far) % ways) for d in range(ways)])]
    all_to_all x5 -> x0, starting transfers between devices: 20 us -> none  [tick_step(): lax.all_to_all(outgoing, 'dom', split_axis=0, concat_axis=0, tiled=True)]
    ppermute x5, starting transfers between devices: 27.9 us -> 34.8 us  [passed_along(): return lax.ppermute(x, axis, pairs)]
    select_n x10, other arithmetic: 4.02 us -> 0.49 us  [take_rows(): picked = jnp.take(matrix, indices.reshape(-1), axis=0)]
    dot_general x2, matrix products: 1.09 us -> 3.26 us  [combine_tiles(): jnp.einsum('rtij,rtjf->rif', tile_weights, gathered, preferred_element_ty...]
    cond x4, local copies, waits for them, and re-layouts: 1.75 us -> 0.01 us
  transfers between devices with their start and end apart: 10 -> 40, of which waited for: 10 -> 21; matrix products, arithmetic and copies ran while one was open for 0% -> 0% of each run, Pallas kernels for 0% -> 0%
where the time goes in v1:
time: 147 us
  starting transfers between devices  71.9 us (49%)
  waiting for transfers between devices  52 us (35%)
  other arithmetic  10.7 us (7%)
  local copies, waits for them, and re-layouts  6.32 us (4%)
  matrix products  4.76 us (3%)
    ppermute x35, starting transfers between devices, exchange_directly(): lax.ppermute(sent, axis, [(d, (d + far) % ways) for d in range(ways)])  37.1 us
    ppermute x5, starting transfers between devices, passed_along(): return lax.ppermute(x, axis, pairs)  34.8 us
    ppermute x5, waiting for transfers between devices, passed_along(): return lax.ppermute(x, axis, pairs)  30.5 us
    ppermute x35, waiting for transfers between devices, exchange_directly(): lax.ppermute(sent, axis, [(d, (d + far) % ways) for d in range(ways)])  21.5 us
    select_n x5, other arithmetic, tick_step(): current = jnp.where(section_pos == 0, initial, received)  5.59 us
    gather x5, local copies, waits for them, and re-layouts, take_rows(): picked = jnp.take(matrix, indices.reshape(-1), axis=0)  4.31 us
    and x5, other arithmetic, take_rows(): picked = jnp.take(matrix, indices.reshape(-1), axis=0)  3.47 us
    dot_general x2, matrix products, combine_tiles(): jnp.einsum('rtij,rtjf->rif', tile_weights, gathered, preferred_element_ty...  3.26 us
  transfers between devices with their start and end apart: 40, of which 21 were waited for; matrix products, arithmetic and copies ran while one was open for 0% of the time, Pallas kernels for 0%

profile of v1, /device:TPU:1, one launch (start us, length us, event | category | flops | bytes accessed | tf_op | source)
XLA Modules:
  0.0 146.5 jit_solution(2590009291000908917)
XLA Ops:
  0.3 145.3 %while.19 = (s32[]{:T(128)}, bf16[256,1024]{1,0:T(8,128)(2,1)S(1)}, bf16[2,256,1024]{2,1,0:T(8,128)(2,1)S(1)}, s32[]{:T(128)}, pred[]{:T(512)}, /*index=5*/bf16[...) while((s32[]{:T(128)}, bf16[256,1024]{1,0:T(8,128)(2,1)S(1)}, ...), condition=%wide.region_3.5_spmd, body=%wide.region_0.4_spmd.sunk | while | flops 810027200 | bytes 25766064 | solution.py:110
  1.1 1.1 broadcast_select_fusion.4
  3.4 5.1 %collective-permute-start = (bf16[1,16,1024]{2,1,0:T(8,128)(2,1)S(1)}, bf16[1,16,1024]{2,1,0:T(8,128)(2,1)S(1)}, u32[]{:S(2)}, u32[]{:S(2)}) collective-permute-start(bf16[1,16,1024]{2,1,0:T(8,128)(2,1)S(1)} %get-tuple-element.459), channel_id=1, source_target_pairs={{0,7},{1,0},{2,1},{3,2},{4,3},{5,4},{6,5},{7,6},{8,15},{9,8},{10,9... | collective-permute-start | bytes 98312 | tf_op jit(solution)/shard_map/while/body/eval_jaxpr/ppermute | solution.py:17
  8.7 2.4 %collective-permute-start.3 = (bf16[1,16,1024]{2,1,0:T(8,128)(2,1)S(1)}, bf16[1,16,1024]{2,1,0:T(8,128)(2,1)S(1)}, u32[]{:S(2)}, u32[]{:S(2)}) collective-permute-start(bf16[1,16,1024]{2,1,0:T(8,128)(2,1)S(1)} %get-tuple-element.462), channel_id=1, source_target_pairs={{0,4},{1,5},{2,6},{3,7},{4,0},{5,1},{6,2},{7,3},{8,12},{9,13},{10,... | collective-permute-start | bytes 98312 | tf_op jit(solution)/shard_map/while/body/eval_jaxpr/ppermute | solution.py:17
  11.1 1.3 collective-permute-start.5
  12.4 1.1 collective-permute-start.6
  13.6 2.3 %collective-permute-done.4 = bf16[1,16,1024]{2,1,0:T(8,128)(2,1)S(1)} collective-permute-done((bf16[1,16,1024]{2,1,0:T(8,128)(2,1)S(1)}, bf16[1,16,1024]{2,1,0:T(8,128)(2,1)S(1)}, u32[]{:S(2)}, u32[]{:S(2)}) %collective-permute-start.4) | collective-permute-done | bytes 32800 | tf_op jit(solution)/shard_map/while/body/eval_jaxpr/ppermute | solution.py:17
  15.8 1.1 collective-permute-done.5
  18.0 6.5 %collective-permute-start.7 = (bf16[256,1024]{1,0:T(8,128)(2,1)S(1)}, bf16[256,1024]{1,0:T(8,128)(2,1)S(1)}, u32[]{:S(2)}, u32[]{:S(2)}) collective-permute-start(bf16[256,1024]{1,0:T(8,128)(2,1)S(1)} %get-tuple-element.467), channel_id=1, source_target_pairs={{0,8},{8,16},{16,24},{1,9},{9,17},{17,25},{2,10},{10,18},{18,26},{... | collective-permute-start | bytes 1572872 | tf_op jit(solution)/shard_map/while/body/eval_jaxpr/ppermute | solution.py:25
  24.5 6.1 %collective-permute-done.7 = bf16[256,1024]{1,0:T(8,128)(2,1)S(1)} collective-permute-done((bf16[256,1024]{1,0:T(8,128)(2,1)S(1)}, bf16[256,1024]{1,0:T(8,128)(2,1)S(1)}, u32[]{:S(2)}, u32[]{:S(2)}) %collective-permute-start.7) | collective-permute-done | bytes 524320 | tf_op jit(solution)/shard_map/while/body/eval_jaxpr/ppermute | solution.py:25
  31.4 1.1 broadcast_select_fusion.4
  33.7 1.1 collective-permute-start.1
  34.9 1.5 collective-permute-start.2
  36.3 1.9 %collective-permute-start.3 = (bf16[1,16,1024]{2,1,0:T(8,128)(2,1)S(1)}, bf16[1,16,1024]{2,1,0:T(8,128)(2,1)S(1)}, u32[]{:S(2)}, u32[]{:S(2)}) collective-permute-start(bf16[1,16,1024]{2,1,0:T(8,128)(2,1)S(1)} %get-tuple-element.462), channel_id=1, source_target_pairs={{0,4},{1,5},{2,6},{3,7},{4,0},{5,1},{6,2},{7,3},{8,12},{9,13},{10,... | collective-permute-start | bytes 98312 | tf_op jit(solution)/shard_map/while/body/eval_jaxpr/ppermute | solution.py:17
  38.2 1.7 %collective-permute-start.5 = (bf16[1,16,1024]{2,1,0:T(8,128)(2,1)S(1)}, bf16[1,16,1024]{2,1,0:T(8,128)(2,1)S(1)}, u32[]{:S(2)}, u32[]{:S(2)}) collective-permute-start(bf16[1,16,1024]{2,1,0:T(8,128)(2,1)S(1)} %get-tuple-element.464), channel_id=1, source_target_pairs={{0,2},{1,3},{2,4},{3,5},{4,6},{5,7},{6,0},{7,1},{8,10},{9,11},{10,... | collective-permute-start | bytes 98312 | tf_op jit(solution)/shard_map/while/body/eval_jaxpr/ppermute | solution.py:17
  40.0 1.4 collective-permute-start.6
  41.5 1.2 collective-permute-done.4
  42.8 2.6 %collective-permute-done.6 = bf16[1,16,1024]{2,1,0:T(8,128)(2,1)S(1)} collective-permute-done((bf16[1,16,1024]{2,1,0:T(8,128)(2,1)S(1)}, bf16[1,16,1024]{2,1,0:T(8,128)(2,1)S(1)}, u32[]{:S(2)}, u32[]{:S(2)}) %collective-permute-start.6) | collective-permute-done | bytes 32800 | tf_op jit(solution)/shard_map/while/body/eval_jaxpr/ppermute | solution.py:17
  45.5 2.7 %conditional.2 = (bf16[256,1024]{1,0:T(8,128)(2,1)S(1)}, bf16[2,256,1024]{2,1,0:T(8,128)(2,1)S(1)}) conditional(s32[]{:T(128)} %convert_element_type.41, bf16[2,256,1024]{2,1,0:T(8,128)(2,1)S(1)} %get-tuple-element.493, (f32[]{:T(128)}, bf16[2,2,4,128,128]{4,3,2,1,0:T(8,128)(2,1)}, s32[]{:T(128)}, s32[2,2,4]{2,1,0:T(2,128)S(1)}, ...), branch_computations={%region_1.2_spmd, %region_2.3_spmd.clone} | conditional | flops 809238528 | bytes 17302208 | solution.py:95
  45.6 1.6 %fusion.8 = f32[2,128,1024]{2,1,0:T(8,128)S(1)} fusion(pred[2,4]{1,0:T(4,128)(4,1)S(1)} %compare_bitcast_fusion, bf16[128,1024]{1,0:T(8,128)(2,1)S(1)} %bitcast.50, bf16[2,128,1024]{2,1,0:T(8,128)(2,1)S(1)} %bitcast.48, bf16[2,2,4,128,128]{4,3,2,1,0:T(8,128)(2,1)} %get-tuple-element.314, s32[]{:T(128)} %get-tuple-element.315), kind=kOutput, calls=%fused_computation.8 | convolution fusion | flops 269746176 | bytes 2097672 | tf_op jit(solution)/shard_map/while/body/eval_jaxpr/cond/branch_1_fun/rtij,rtjf->rif/dot_general | solution.py:40
  48.1 4.4 %collective-permute-start.7 = (bf16[256,1024]{1,0:T(8,128)(2,1)S(1)}, bf16[256,1024]{1,0:T(8,128)(2,1)S(1)}, u32[]{:S(2)}, u32[]{:S(2)}) collective-permute-start(bf16[256,1024]{1,0:T(8,128)(2,1)S(1)} %get-tuple-element.467), channel_id=1, source_target_pairs={{0,8},{8,16},{16,24},{1,9},{9,17},{17,25},{2,10},{10,18},{18,26},{... | collective-permute-start | bytes 1572872 | tf_op jit(solution)/shard_map/while/body/eval_jaxpr/ppermute | solution.py:25
  52.5 6.1 %collective-permute-done.7 = bf16[256,1024]{1,0:T(8,128)(2,1)S(1)} collective-permute-done((bf16[256,1024]{1,0:T(8,128)(2,1)S(1)}, bf16[256,1024]{1,0:T(8,128)(2,1)S(1)}, u32[]{:S(2)}, u32[]{:S(2)}) %collective-permute-start.7) | collective-permute-done | bytes 524320 | tf_op jit(solution)/shard_map/while/body/eval_jaxpr/ppermute | solution.py:25
  59.4 1.1 broadcast_select_fusion.4
  62.8 2.4 %collective-permute-start.3 = (bf16[1,16,1024]{2,1,0:T(8,128)(2,1)S(1)}, bf16[1,16,1024]{2,1,0:T(8,128)(2,1)S(1)}, u32[]{:S(2)}, u32[]{:S(2)}) collective-permute-start(bf16[1,16,1024]{2,1,0:T(8,128)(2,1)S(1)} %get-tuple-element.462), channel_id=1, source_target_pairs={{0,4},{1,5},{2,6},{3,7},{4,0},{5,1},{6,2},{7,3},{8,12},{9,13},{10,... | collective-permute-start | bytes 98312 | tf_op jit(solution)/shard_map/while/body/eval_jaxpr/ppermute | solution.py:17
  65.4 1.6 %collective-permute-start.5 = (bf16[1,16,1024]{2,1,0:T(8,128)(2,1)S(1)}, bf16[1,16,1024]{2,1,0:T(8,128)(2,1)S(1)}, u32[]{:S(2)}, u32[]{:S(2)}) collective-permute-start(bf16[1,16,1024]{2,1,0:T(8,128)(2,1)S(1)} %get-tuple-element.464), channel_id=1, source_target_pairs={{0,2},{1,3},{2,4},{3,5},{4,6},{5,7},{6,0},{7,1},{8,10},{9,11},{10,... | collective-permute-start | bytes 98312 | tf_op jit(solution)/shard_map/while/body/eval_jaxpr/ppermute | solution.py:17
  68.0 1.9 %collective-permute-done.4 = bf16[1,16,1024]{2,1,0:T(8,128)(2,1)S(1)} collective-permute-done((bf16[1,16,1024]{2,1,0:T(8,128)(2,1)S(1)}, bf16[1,16,1024]{2,1,0:T(8,128)(2,1)S(1)}, u32[]{:S(2)}, u32[]{:S(2)}) %collective-permute-start.4) | collective-permute-done | bytes 32800 | tf_op jit(solution)/shard_map/while/body/eval_jaxpr/ppermute | solution.py:17
  70.4 2.1 %collective-permute-done.6 = bf16[1,16,1024]{2,1,0:T(8,128)(2,1)S(1)} collective-permute-done((bf16[1,16,1024]{2,1,0:T(8,128)(2,1)S(1)}, bf16[1,16,1024]{2,1,0:T(8,128)(2,1)S(1)}, u32[]{:S(2)}, u32[]{:S(2)}) %collective-permute-start.6) | collective-permute-done | bytes 32800 | tf_op jit(solution)/shard_map/while/body/eval_jaxpr/ppermute | solution.py:17
  72.5 2.7 %conditional.2 = (bf16[256,1024]{1,0:T(8,128)(2,1)S(1)}, bf16[2,256,1024]{2,1,0:T(8,128)(2,1)S(1)}) conditional(s32[]{:T(128)} %convert_element_type.41, bf16[2,256,1024]{2,1,0:T(8,128)(2,1)S(1)} %get-tuple-element.493, (f32[]{:T(128)}, bf16[2,2,4,128,128]{4,3,2,1,0:T(8,128)(2,1)}, s32[]{:T(128)}, s32[2,2,4]{2,1,0:T(2,128)S(1)}, ...), branch_computations={%region_1.2_spmd, %region_2.3_spmd.clone} | conditional | flops 809238528 | bytes 17302208 | solution.py:95
  72.6 1.6 %fusion.8 = f32[2,128,1024]{2,1,0:T(8,128)S(1)} fusion(pred[2,4]{1,0:T(4,128)(4,1)S(1)} %compare_bitcast_fusion, bf16[128,1024]{1,0:T(8,128)(2,1)S(1)} %bitcast.50, bf16[2,128,1024]{2,1,0:T(8,128)(2,1)S(1)} %bitcast.48, bf16[2,2,4,128,128]{4,3,2,1,0:T(8,128)(2,1)} %get-tuple-element.314, s32[]{:T(128)} %get-tuple-element.315), kind=kOutput, calls=%fused_computation.8 | convolution fusion | flops 269746176 | bytes 2097672 | tf_op jit(solution)/shard_map/while/body/eval_jaxpr/cond/branch_1_fun/rtij,rtjf->rif/dot_general | solution.py:40
  75.2 7.2 %collective-permute-start.7 = (bf16[256,1024]{1,0:T(8,128)(2,1)S(1)}, bf16[256,1024]{1,0:T(8,128)(2,1)S(1)}, u32[]{:S(2)}, u32[]{:S(2)}) collective-permute-start(bf16[256,1024]{1,0:T(8,128)(2,1)S(1)} %get-tuple-element.467), channel_id=1, source_target_pairs={{0,8},{8,16},{16,24},{1,9},{9,17},{17,25},{2,10},{10,18},{18,26},{... | collective-permute-start | bytes 1572872 | tf_op jit(solution)/shard_map/while/body/eval_jaxpr/ppermute | solution.py:25
  82.4 6.1 %collective-permute-done.7 = bf16[256,1024]{1,0:T(8,128)(2,1)S(1)} collective-permute-done((bf16[256,1024]{1,0:T(8,128)(2,1)S(1)}, bf16[256,1024]{1,0:T(8,128)(2,1)S(1)}, u32[]{:S(2)}, u32[]{:S(2)}) %collective-permute-start.7) | collective-permute-done | bytes 524320 | tf_op jit(solution)/shard_map/while/body/eval_jaxpr/ppermute | solution.py:25
  89.3 1.1 broadcast_select_fusion.4
  91.6 1.4 collective-permute-start.1
  93.1 2.1 %collective-permute-start.3 = (bf16[1,16,1024]{2,1,0:T(8,128)(2,1)S(1)}, bf16[1,16,1024]{2,1,0:T(8,128)(2,1)S(1)}, u32[]{:S(2)}, u32[]{:S(2)}) collective-permute-start(bf16[1,16,1024]{2,1,0:T(8,128)(2,1)S(1)} %get-tuple-element.462), channel_id=1, source_target_pairs={{0,4},{1,5},{2,6},{3,7},{4,0},{5,1},{6,2},{7,3},{8,12},{9,13},{10,... | collective-permute-start | bytes 98312 | tf_op jit(solution)/shard_map/while/body/eval_jaxpr/ppermute | solution.py:17
  95.5 1.2 collective-permute-start.5
  96.7 1.4 collective-permute-start.6
  98.1 1.7 %collective-permute-done.4 = bf16[1,16,1024]{2,1,0:T(8,128)(2,1)S(1)} collective-permute-done((bf16[1,16,1024]{2,1,0:T(8,128)(2,1)S(1)}, bf16[1,16,1024]{2,1,0:T(8,128)(2,1)S(1)}, u32[]{:S(2)}, u32[]{:S(2)}) %collective-permute-start.4) | collective-permute-done | bytes 32800 | tf_op jit(solution)/shard_map/while/body/eval_jaxpr/ppermute | solution.py:17
  100.2 2.0 %collective-permute-done.6 = bf16[1,16,1024]{2,1,0:T(8,128)(2,1)S(1)} collective-permute-done((bf16[1,16,1024]{2,1,0:T(8,128)(2,1)S(1)}, bf16[1,16,1024]{2,1,0:T(8,128)(2,1)S(1)}, u32[]{:S(2)}, u32[]{:S(2)}) %collective-permute-start.6) | collective-permute-done | bytes 32800 | tf_op jit(solution)/shard_map/while/body/eval_jaxpr/ppermute | solution.py:17
  102.3 9.5 %collective-permute-start.7 = (bf16[256,1024]{1,0:T(8,128)(2,1)S(1)}, bf16[256,1024]{1,0:T(8,128)(2,1)S(1)}, u32[]{:S(2)}, u32[]{:S(2)}) collective-permute-start(bf16[256,1024]{1,0:T(8,128)(2,1)S(1)} %get-tuple-element.467), channel_id=1, source_target_pairs={{0,8},{8,16},{16,24},{1,9},{9,17},{17,25},{2,10},{10,18},{18,26},{... | collective-permute-start | bytes 1572872 | tf_op jit(solution)/shard_map/while/body/eval_jaxpr/ppermute | solution.py:25
  111.8 6.1 %collective-permute-done.7 = bf16[256,1024]{1,0:T(8,128)(2,1)S(1)} collective-permute-done((bf16[256,1024]{1,0:T(8,128)(2,1)S(1)}, bf16[256,1024]{1,0:T(8,128)(2,1)S(1)}, u32[]{:S(2)}, u32[]{:S(2)}) %collective-permute-start.7) | collective-permute-done | bytes 524320 | tf_op jit(solution)/shard_map/while/body/eval_jaxpr/ppermute | solution.py:25
  118.7 1.1 broadcast_select_fusion.4
  121.3 1.7 %collective-permute-start.1 = (bf16[1,16,1024]{2,1,0:T(8,128)(2,1)S(1)}, bf16[1,16,1024]{2,1,0:T(8,128)(2,1)S(1)}, u32[]{:S(2)}, u32[]{:S(2)}) collective-permute-start(bf16[1,16,1024]{2,1,0:T(8,128)(2,1)S(1)} %get-tuple-element.460), channel_id=1, source_target_pairs={{0,6},{1,7},{2,0},{3,1},{4,2},{5,3},{6,4},{7,5},{8,14},{9,15},{10,... | collective-permute-start | bytes 98312 | tf_op jit(solution)/shard_map/while/body/eval_jaxpr/ppermute | solution.py:17
  123.3 1.9 %collective-permute-start.3 = (bf16[1,16,1024]{2,1,0:T(8,128)(2,1)S(1)}, bf16[1,16,1024]{2,1,0:T(8,128)(2,1)S(1)}, u32[]{:S(2)}, u32[]{:S(2)}) collective-permute-start(bf16[1,16,1024]{2,1,0:T(8,128)(2,1)S(1)} %get-tuple-element.462), channel_id=1, source_target_pairs={{0,4},{1,5},{2,6},{3,7},{4,0},{5,1},{6,2},{7,3},{8,12},{9,13},{10,... | collective-permute-start | bytes 98312 | tf_op jit(solution)/shard_map/while/body/eval_jaxpr/ppermute | solution.py:17
  125.4 1.2 collective-permute-start.5
  127.7 2.1 %collective-permute-done.4 = bf16[1,16,1024]{2,1,0:T(8,128)(2,1)S(1)} collective-permute-done((bf16[1,16,1024]{2,1,0:T(8,128)(2,1)S(1)}, bf16[1,16,1024]{2,1,0:T(8,128)(2,1)S(1)}, u32[]{:S(2)}, u32[]{:S(2)}) %collective-permute-start.4) | collective-permute-done | bytes 32800 | tf_op jit(solution)/shard_map/while/body/eval_jaxpr/ppermute | solution.py:17
  129.9 2.1 %collective-permute-done.6 = bf16[1,16,1024]{2,1,0:T(8,128)(2,1)S(1)} collective-permute-done((bf16[1,16,1024]{2,1,0:T(8,128)(2,1)S(1)}, bf16[1,16,1024]{2,1,0:T(8,128)(2,1)S(1)}, u32[]{:S(2)}, u32[]{:S(2)}) %collective-permute-start.6) | collective-permute-done | bytes 32800 | tf_op jit(solution)/shard_map/while/body/eval_jaxpr/ppermute | solution.py:17
  132.2 7.2 %collective-permute-start.7 = (bf16[256,1024]{1,0:T(8,128)(2,1)S(1)}, bf16[256,1024]{1,0:T(8,128)(2,1)S(1)}, u32[]{:S(2)}, u32[]{:S(2)}) collective-permute-start(bf16[256,1024]{1,0:T(8,128)(2,1)S(1)} %get-tuple-element.467), channel_id=1, source_target_pairs={{0,8},{8,16},{16,24},{1,9},{9,17},{17,25},{2,10},{10,18},{18,26},{... | collective-permute-start | bytes 1572872 | tf_op jit(solution)/shard_map/while/body/eval_jaxpr/ppermute | solution.py:25
  139.5 6.1 %collective-permute-done.7 = bf16[256,1024]{1,0:T(8,128)(2,1)S(1)} collective-permute-done((bf16[256,1024]{1,0:T(8,128)(2,1)S(1)}, bf16[256,1024]{1,0:T(8,128)(2,1)S(1)}, u32[]{:S(2)}, u32[]{:S(2)}) %collective-permute-start.7) | collective-permute-done | bytes 524320 | tf_op jit(solution)/shard_map/while/body/eval_jaxpr/ppermute | solution.py:25
  (159 shorter events, 20.1 us)
Async XLA Ops:
  2.2 15.7 %copy-start.1 = (s32[2,2,4]{2,1,0:T(2,128)S(1)}, s32[2,2,4]{2,1,0:T(2,128)}, u32[]{:S(2)}) copy-start(s32[2,2,4]{2,1,0:T(2,128)} %get-tuple-element.518) | copy-start | bytes 196 | tf_op jit(solution)/shard_map/while
  3.4 7.7 %collective-permute-start = (bf16[1,16,1024]{2,1,0:T(8,128)(2,1)S(1)}, bf16[1,16,1024]{2,1,0:T(8,128)(2,1)S(1)}, u32[]{:S(2)}, u32[]{:S(2)}) collective-permute-start(bf16[1,16,1024]{2,1,0:T(8,128)(2,1)S(1)} %get-tuple-element.459), channel_id=1, source_target_pairs={{0,7},{1,0},{2,1},{3,2},{4,3},{5,4},{6,5},{7,6},{8,15},{9,8},{10,9... | collective-permute-start | bytes 98312 | tf_op jit(solution)/shard_map/while/body/eval_jaxpr/ppermute | solution.py:17
  8.5 3.9 %collective-permute-start.1 = (bf16[1,16,1024]{2,1,0:T(8,128)(2,1)S(1)}, bf16[1,16,1024]{2,1,0:T(8,128)(2,1)S(1)}, u32[]{:S(2)}, u32[]{:S(2)}) collective-permute-start(bf16[1,16,1024]{2,1,0:T(8,128)(2,1)S(1)} %get-tuple-element.460), channel_id=1, source_target_pairs={{0,6},{1,7},{2,0},{3,1},{4,2},{5,3},{6,4},{7,5},{8,14},{9,15},{10,... | collective-permute-start | bytes 98312 | tf_op jit(solution)/shard_map/while/body/eval_jaxpr/ppermute | solution.py:17
  8.7 4.9 %collective-permute-start.2 = (bf16[1,16,1024]{2,1,0:T(8,128)(2,1)S(1)}, bf16[1,16,1024]{2,1,0:T(8,128)(2,1)S(1)}, u32[]{:S(2)}, u32[]{:S(2)}) collective-permute-start(bf16[1,16,1024]{2,1,0:T(8,128)(2,1)S(1)} %get-tuple-element.461), channel_id=1, source_target_pairs={{0,5},{1,6},{2,7},{3,0},{4,1},{5,2},{6,3},{7,4},{8,13},{9,14},{10,... | collective-permute-start | bytes 98312 | tf_op jit(solution)/shard_map/while/body/eval_jaxpr/ppermute | solution.py:17
  8.7 4.9 %collective-permute-start.3 = (bf16[1,16,1024]{2,1,0:T(8,128)(2,1)S(1)}, bf16[1,16,1024]{2,1,0:T(8,128)(2,1)S(1)}, u32[]{:S(2)}, u32[]{:S(2)}) collective-permute-start(bf16[1,16,1024]{2,1,0:T(8,128)(2,1)S(1)} %get-tuple-element.462), channel_id=1, source_target_pairs={{0,4},{1,5},{2,6},{3,7},{4,0},{5,1},{6,2},{7,3},{8,12},{9,13},{10,... | collective-permute-start | bytes 98312 | tf_op jit(solution)/shard_map/while/body/eval_jaxpr/ppermute | solution.py:17
  11.1 4.7 %collective-permute-start.4 = (bf16[1,16,1024]{2,1,0:T(8,128)(2,1)S(1)}, bf16[1,16,1024]{2,1,0:T(8,128)(2,1)S(1)}, u32[]{:S(2)}, u32[]{:S(2)}) collective-permute-start(bf16[1,16,1024]{2,1,0:T(8,128)(2,1)S(1)} %get-tuple-element.463), channel_id=1, source_target_pairs={{0,3},{1,4},{2,5},{3,6},{4,7},{5,0},{6,1},{7,2},{8,11},{9,12},{10,... | collective-permute-start | bytes 98312 | tf_op jit(solution)/shard_map/while/body/eval_jaxpr/ppermute | solution.py:17
  11.1 5.8 %collective-permute-start.5 = (bf16[1,16,1024]{2,1,0:T(8,128)(2,1)S(1)}, bf16[1,16,1024]{2,1,0:T(8,128)(2,1)S(1)}, u32[]{:S(2)}, u32[]{:S(2)}) collective-permute-start(bf16[1,16,1024]{2,1,0:T(8,128)(2,1)S(1)} %get-tuple-element.464), channel_id=1, source_target_pairs={{0,2},{1,3},{2,4},{3,5},{4,6},{5,7},{6,0},{7,1},{8,10},{9,11},{10,... | collective-permute-start | bytes 98312 | tf_op jit(solution)/shard_map/while/body/eval_jaxpr/ppermute | solution.py:17
  12.4 5.5 %collective-permute-start.6 = (bf16[1,16,1024]{2,1,0:T(8,128)(2,1)S(1)}, bf16[1,16,1024]{2,1,0:T(8,128)(2,1)S(1)}, u32[]{:S(2)}, u32[]{:S(2)}) collective-permute-start(bf16[1,16,1024]{2,1,0:T(8,128)(2,1)S(1)} %get-tuple-element.465), channel_id=1, source_target_pairs={{0,1},{1,2},{2,3},{3,4},{4,5},{5,6},{6,7},{7,0},{8,9},{9,10},{10,1... | collective-permute-start | bytes 98312 | tf_op jit(solution)/shard_map/while/body/eval_jaxpr/ppermute | solution.py:17
  18.0 12.6 %collective-permute-start.7 = (bf16[256,1024]{1,0:T(8,128)(2,1)S(1)}, bf16[256,1024]{1,0:T(8,128)(2,1)S(1)}, u32[]{:S(2)}, u32[]{:S(2)}) collective-permute-start(bf16[256,1024]{1,0:T(8,128)(2,1)S(1)} %get-tuple-element.467), channel_id=1, source_target_pairs={{0,8},{8,16},{16,24},{1,9},{9,17},{17,25},{2,10},{10,18},{18,26},{... | collective-permute-start | bytes 1572872 | tf_op jit(solution)/shard_map/while/body/eval_jaxpr/ppermute | solution.py:25
  32.6 12.9 %copy-start.1 = (s32[2,2,4]{2,1,0:T(2,128)S(1)}, s32[2,2,4]{2,1,0:T(2,128)}, u32[]{:S(2)}) copy-start(s32[2,2,4]{2,1,0:T(2,128)} %get-tuple-element.518) | copy-start | bytes 196 | tf_op jit(solution)/shard_map/while
  33.7 4.5 %collective-permute-start = (bf16[1,16,1024]{2,1,0:T(8,128)(2,1)S(1)}, bf16[1,16,1024]{2,1,0:T(8,128)(2,1)S(1)}, u32[]{:S(2)}, u32[]{:S(2)}) collective-permute-start(bf16[1,16,1024]{2,1,0:T(8,128)(2,1)S(1)} %get-tuple-element.459), channel_id=1, source_target_pairs={{0,7},{1,0},{2,1},{3,2},{4,3},{5,4},{6,5},{7,6},{8,15},{9,8},{10,9... | collective-permute-start | bytes 98312 | tf_op jit(solution)/shard_map/while/body/eval_jaxpr/ppermute | solution.py:17
  33.7 6.2 %collective-permute-start.1 = (bf16[1,16,1024]{2,1,0:T(8,128)(2,1)S(1)}, bf16[1,16,1024]{2,1,0:T(8,128)(2,1)S(1)}, u32[]{:S(2)}, u32[]{:S(2)}) collective-permute-start(bf16[1,16,1024]{2,1,0:T(8,128)(2,1)S(1)} %get-tuple-element.460), channel_id=1, source_target_pairs={{0,6},{1,7},{2,0},{3,1},{4,2},{5,3},{6,4},{7,5},{8,14},{9,15},{10,... | collective-permute-start | bytes 98312 | tf_op jit(solution)/shard_map/while/body/eval_jaxpr/ppermute | solution.py:17
  34.9 6.5 %collective-permute-start.2 = (bf16[1,16,1024]{2,1,0:T(8,128)(2,1)S(1)}, bf16[1,16,1024]{2,1,0:T(8,128)(2,1)S(1)}, u32[]{:S(2)}, u32[]{:S(2)}) collective-permute-start(bf16[1,16,1024]{2,1,0:T(8,128)(2,1)S(1)} %get-tuple-element.461), channel_id=1, source_target_pairs={{0,5},{1,6},{2,7},{3,0},{4,1},{5,2},{6,3},{7,4},{8,13},{9,14},{10,... | collective-permute-start | bytes 98312 | tf_op jit(solution)/shard_map/while/body/eval_jaxpr/ppermute | solution.py:17
  36.3 5.2 %collective-permute-start.3 = (bf16[1,16,1024]{2,1,0:T(8,128)(2,1)S(1)}, bf16[1,16,1024]{2,1,0:T(8,128)(2,1)S(1)}, u32[]{:S(2)}, u32[]{:S(2)}) collective-permute-start(bf16[1,16,1024]{2,1,0:T(8,128)(2,1)S(1)} %get-tuple-element.462), channel_id=1, source_target_pairs={{0,4},{1,5},{2,6},{3,7},{4,0},{5,1},{6,2},{7,3},{8,12},{9,13},{10,... | collective-permute-start | bytes 98312 | tf_op jit(solution)/shard_map/while/body/eval_jaxpr/ppermute | solution.py:17
  38.2 4.6 %collective-permute-start.4 = (bf16[1,16,1024]{2,1,0:T(8,128)(2,1)S(1)}, bf16[1,16,1024]{2,1,0:T(8,128)(2,1)S(1)}, u32[]{:S(2)}, u32[]{:S(2)}) collective-permute-start(bf16[1,16,1024]{2,1,0:T(8,128)(2,1)S(1)} %get-tuple-element.463), channel_id=1, source_target_pairs={{0,3},{1,4},{2,5},{3,6},{4,7},{5,0},{6,1},{7,2},{8,11},{9,12},{10,... | collective-permute-start | bytes 98312 | tf_op jit(solution)/shard_map/while/body/eval_jaxpr/ppermute | solution.py:17
  38.2 4.6 %collective-permute-start.5 = (bf16[1,16,1024]{2,1,0:T(8,128)(2,1)S(1)}, bf16[1,16,1024]{2,1,0:T(8,128)(2,1)S(1)}, u32[]{:S(2)}, u32[]{:S(2)}) collective-permute-start(bf16[1,16,1024]{2,1,0:T(8,128)(2,1)S(1)} %get-tuple-element.464), channel_id=1, source_target_pairs={{0,2},{1,3},{2,4},{3,5},{4,6},{5,7},{6,0},{7,1},{8,10},{9,11},{10,... | collective-permute-start | bytes 98312 | tf_op jit(solution)/shard_map/while/body/eval_jaxpr/ppermute | solution.py:17
  40.0 5.5 %collective-permute-start.6 = (bf16[1,16,1024]{2,1,0:T(8,128)(2,1)S(1)}, bf16[1,16,1024]{2,1,0:T(8,128)(2,1)S(1)}, u32[]{:S(2)}, u32[]{:S(2)}) collective-permute-start(bf16[1,16,1024]{2,1,0:T(8,128)(2,1)S(1)} %get-tuple-element.465), channel_id=1, source_target_pairs={{0,1},{1,2},{2,3},{3,4},{4,5},{5,6},{6,7},{7,0},{8,9},{9,10},{10,1... | collective-permute-start | bytes 98312 | tf_op jit(solution)/shard_map/while/body/eval_jaxpr/ppermute | solution.py:17
  45.6 1.8 %copy-start.2 = (bf16[1024,1024]{1,0:T(8,128)(2,1)S(1)}, bf16[1024,1024]{1,0:T(8,128)(2,1)}, u32[]{:S(2)}) copy-start(bf16[1024,1024]{1,0:T(8,128)(2,1)} %get-tuple-element.319) | copy-start | bytes 6291460 | tf_op jit(solution)/shard_map/while/body/eval_jaxpr/cond
  48.1 10.5 %collective-permute-start.7 = (bf16[256,1024]{1,0:T(8,128)(2,1)S(1)}, bf16[256,1024]{1,0:T(8,128)(2,1)S(1)}, u32[]{:S(2)}, u32[]{:S(2)}) collective-permute-start(bf16[256,1024]{1,0:T(8,128)(2,1)S(1)} %get-tuple-element.467), channel_id=1, source_target_pairs={{0,8},{8,16},{16,24},{1,9},{9,17},{17,25},{2,10},{10,18},{18,26},{... | collective-permute-start | bytes 1572872 | tf_op jit(solution)/shard_map/while/body/eval_jaxpr/ppermute | solution.py:25
  60.5 12.0 %copy-start.1 = (s32[2,2,4]{2,1,0:T(2,128)S(1)}, s32[2,2,4]{2,1,0:T(2,128)}, u32[]{:S(2)}) copy-start(s32[2,2,4]{2,1,0:T(2,128)} %get-tuple-element.518) | copy-start | bytes 196 | tf_op jit(solution)/shard_map/while
  61.7 3.8 %collective-permute-start = (bf16[1,16,1024]{2,1,0:T(8,128)(2,1)S(1)}, bf16[1,16,1024]{2,1,0:T(8,128)(2,1)S(1)}, u32[]{:S(2)}, u32[]{:S(2)}) collective-permute-start(bf16[1,16,1024]{2,1,0:T(8,128)(2,1)S(1)} %get-tuple-element.459), channel_id=1, source_target_pairs={{0,7},{1,0},{2,1},{3,2},{4,3},{5,4},{6,5},{7,6},{8,15},{9,8},{10,9... | collective-permute-start | bytes 98312 | tf_op jit(solution)/shard_map/while/body/eval_jaxpr/ppermute | solution.py:17
  61.9 5.1 %collective-permute-start.1 = (bf16[1,16,1024]{2,1,0:T(8,128)(2,1)S(1)}, bf16[1,16,1024]{2,1,0:T(8,128)(2,1)S(1)}, u32[]{:S(2)}, u32[]{:S(2)}) collective-permute-start(bf16[1,16,1024]{2,1,0:T(8,128)(2,1)S(1)} %get-tuple-element.460), channel_id=1, source_target_pairs={{0,6},{1,7},{2,0},{3,1},{4,2},{5,3},{6,4},{7,5},{8,14},{9,15},{10,... | collective-permute-start | bytes 98312 | tf_op jit(solution)/shard_map/while/body/eval_jaxpr/ppermute | solution.py:17
  62.5 5.4 %collective-permute-start.2 = (bf16[1,16,1024]{2,1,0:T(8,128)(2,1)S(1)}, bf16[1,16,1024]{2,1,0:T(8,128)(2,1)S(1)}, u32[]{:S(2)}, u32[]{:S(2)}) collective-permute-start(bf16[1,16,1024]{2,1,0:T(8,128)(2,1)S(1)} %get-tuple-element.461), channel_id=1, source_target_pairs={{0,5},{1,6},{2,7},{3,0},{4,1},{5,2},{6,3},{7,4},{8,13},{9,14},{10,... | collective-permute-start | bytes 98312 | tf_op jit(solution)/shard_map/while/body/eval_jaxpr/ppermute | solution.py:17
  62.8 5.1 %collective-permute-start.3 = (bf16[1,16,1024]{2,1,0:T(8,128)(2,1)S(1)}, bf16[1,16,1024]{2,1,0:T(8,128)(2,1)S(1)}, u32[]{:S(2)}, u32[]{:S(2)}) collective-permute-start(bf16[1,16,1024]{2,1,0:T(8,128)(2,1)S(1)} %get-tuple-element.462), channel_id=1, source_target_pairs={{0,4},{1,5},{2,6},{3,7},{4,0},{5,1},{6,2},{7,3},{8,12},{9,13},{10,... | collective-permute-start | bytes 98312 | tf_op jit(solution)/shard_map/while/body/eval_jaxpr/ppermute | solution.py:17
  65.3 4.6 %collective-permute-start.4 = (bf16[1,16,1024]{2,1,0:T(8,128)(2,1)S(1)}, bf16[1,16,1024]{2,1,0:T(8,128)(2,1)S(1)}, u32[]{:S(2)}, u32[]{:S(2)}) collective-permute-start(bf16[1,16,1024]{2,1,0:T(8,128)(2,1)S(1)} %get-tuple-element.463), channel_id=1, source_target_pairs={{0,3},{1,4},{2,5},{3,6},{4,7},{5,0},{6,1},{7,2},{8,11},{9,12},{10,... | collective-permute-start | bytes 98312 | tf_op jit(solution)/shard_map/while/body/eval_jaxpr/ppermute | solution.py:17
  65.4 5.0 %collective-permute-start.5 = (bf16[1,16,1024]{2,1,0:T(8,128)(2,1)S(1)}, bf16[1,16,1024]{2,1,0:T(8,128)(2,1)S(1)}, u32[]{:S(2)}, u32[]{:S(2)}) collective-permute-start(bf16[1,16,1024]{2,1,0:T(8,128)(2,1)S(1)} %get-tuple-element.464), channel_id=1, source_target_pairs={{0,2},{1,3},{2,4},{3,5},{4,6},{5,7},{6,0},{7,1},{8,10},{9,11},{10,... | collective-permute-start | bytes 98312 | tf_op jit(solution)/shard_map/while/body/eval_jaxpr/ppermute | solution.py:17
  67.0 5.5 %collective-permute-start.6 = (bf16[1,16,1024]{2,1,0:T(8,128)(2,1)S(1)}, bf16[1,16,1024]{2,1,0:T(8,128)(2,1)S(1)}, u32[]{:S(2)}, u32[]{:S(2)}) collective-permute-start(bf16[1,16,1024]{2,1,0:T(8,128)(2,1)S(1)} %get-tuple-element.465), channel_id=1, source_target_pairs={{0,1},{1,2},{2,3},{3,4},{4,5},{5,6},{6,7},{7,0},{8,9},{9,10},{10,1... | collective-permute-start | bytes 98312 | tf_op jit(solution)/shard_map/while/body/eval_jaxpr/ppermute | solution.py:17
  72.6 1.8 %copy-start.2 = (bf16[1024,1024]{1,0:T(8,128)(2,1)S(1)}, bf16[1024,1024]{1,0:T(8,128)(2,1)}, u32[]{:S(2)}) copy-start(bf16[1024,1024]{1,0:T(8,128)(2,1)} %get-tuple-element.319) | copy-start | bytes 6291460 | tf_op jit(solution)/shard_map/while/body/eval_jaxpr/cond
  75.2 13.3 %collective-permute-start.7 = (bf16[256,1024]{1,0:T(8,128)(2,1)S(1)}, bf16[256,1024]{1,0:T(8,128)(2,1)S(1)}, u32[]{:S(2)}, u32[]{:S(2)}) collective-permute-start(bf16[256,1024]{1,0:T(8,128)(2,1)S(1)} %get-tuple-element.467), channel_id=1, source_target_pairs={{0,8},{8,16},{16,24},{1,9},{9,17},{17,25},{2,10},{10,18},{18,26},{... | collective-permute-start | bytes 1572872 | tf_op jit(solution)/shard_map/while/body/eval_jaxpr/ppermute | solution.py:25
  90.4 11.7 %copy-start.1 = (s32[2,2,4]{2,1,0:T(2,128)S(1)}, s32[2,2,4]{2,1,0:T(2,128)}, u32[]{:S(2)}) copy-start(s32[2,2,4]{2,1,0:T(2,128)} %get-tuple-element.518) | copy-start | bytes 196 | tf_op jit(solution)/shard_map/while
  91.6 3.9 %collective-permute-start = (bf16[1,16,1024]{2,1,0:T(8,128)(2,1)S(1)}, bf16[1,16,1024]{2,1,0:T(8,128)(2,1)S(1)}, u32[]{:S(2)}, u32[]{:S(2)}) collective-permute-start(bf16[1,16,1024]{2,1,0:T(8,128)(2,1)S(1)} %get-tuple-element.459), channel_id=1, source_target_pairs={{0,7},{1,0},{2,1},{3,2},{4,3},{5,4},{6,5},{7,6},{8,15},{9,8},{10,9... | collective-permute-start | bytes 98312 | tf_op jit(solution)/shard_map/while/body/eval_jaxpr/ppermute | solution.py:17
  91.6 5.0 %collective-permute-start.1 = (bf16[1,16,1024]{2,1,0:T(8,128)(2,1)S(1)}, bf16[1,16,1024]{2,1,0:T(8,128)(2,1)S(1)}, u32[]{:S(2)}, u32[]{:S(2)}) collective-permute-start(bf16[1,16,1024]{2,1,0:T(8,128)(2,1)S(1)} %get-tuple-element.460), channel_id=1, source_target_pairs={{0,6},{1,7},{2,0},{3,1},{4,2},{5,3},{6,4},{7,5},{8,14},{9,15},{10,... | collective-permute-start | bytes 98312 | tf_op jit(solution)/shard_map/while/body/eval_jaxpr/ppermute | solution.py:17
  93.1 5.0 %collective-permute-start.2 = (bf16[1,16,1024]{2,1,0:T(8,128)(2,1)S(1)}, bf16[1,16,1024]{2,1,0:T(8,128)(2,1)S(1)}, u32[]{:S(2)}, u32[]{:S(2)}) collective-permute-start(bf16[1,16,1024]{2,1,0:T(8,128)(2,1)S(1)} %get-tuple-element.461), channel_id=1, source_target_pairs={{0,5},{1,6},{2,7},{3,0},{4,1},{5,2},{6,3},{7,4},{8,13},{9,14},{10,... | collective-permute-start | bytes 98312 | tf_op jit(solution)/shard_map/while/body/eval_jaxpr/ppermute | solution.py:17
  93.1 5.0 %collective-permute-start.3 = (bf16[1,16,1024]{2,1,0:T(8,128)(2,1)S(1)}, bf16[1,16,1024]{2,1,0:T(8,128)(2,1)S(1)}, u32[]{:S(2)}, u32[]{:S(2)}) collective-permute-start(bf16[1,16,1024]{2,1,0:T(8,128)(2,1)S(1)} %get-tuple-element.462), channel_id=1, source_target_pairs={{0,4},{1,5},{2,6},{3,7},{4,0},{5,1},{6,2},{7,3},{8,12},{9,13},{10,... | collective-permute-start | bytes 98312 | tf_op jit(solution)/shard_map/while/body/eval_jaxpr/ppermute | solution.py:17
  95.2 4.6 %collective-permute-start.4 = (bf16[1,16,1024]{2,1,0:T(8,128)(2,1)S(1)}, bf16[1,16,1024]{2,1,0:T(8,128)(2,1)S(1)}, u32[]{:S(2)}, u32[]{:S(2)}) collective-permute-start(bf16[1,16,1024]{2,1,0:T(8,128)(2,1)S(1)} %get-tuple-element.463), channel_id=1, source_target_pairs={{0,3},{1,4},{2,5},{3,6},{4,7},{5,0},{6,1},{7,2},{8,11},{9,12},{10,... | collective-permute-start | bytes 98312 | tf_op jit(solution)/shard_map/while/body/eval_jaxpr/ppermute | solution.py:17
  95.5 4.7 %collective-permute-start.5 = (bf16[1,16,1024]{2,1,0:T(8,128)(2,1)S(1)}, bf16[1,16,1024]{2,1,0:T(8,128)(2,1)S(1)}, u32[]{:S(2)}, u32[]{:S(2)}) collective-permute-start(bf16[1,16,1024]{2,1,0:T(8,128)(2,1)S(1)} %get-tuple-element.464), channel_id=1, source_target_pairs={{0,2},{1,3},{2,4},{3,5},{4,6},{5,7},{6,0},{7,1},{8,10},{9,11},{10,... | collective-permute-start | bytes 98312 | tf_op jit(solution)/shard_map/while/body/eval_jaxpr/ppermute | solution.py:17
  96.7 5.5 %collective-permute-start.6 = (bf16[1,16,1024]{2,1,0:T(8,128)(2,1)S(1)}, bf16[1,16,1024]{2,1,0:T(8,128)(2,1)S(1)}, u32[]{:S(2)}, u32[]{:S(2)}) collective-permute-start(bf16[1,16,1024]{2,1,0:T(8,128)(2,1)S(1)} %get-tuple-element.465), channel_id=1, source_target_pairs={{0,1},{1,2},{2,3},{3,4},{4,5},{5,6},{6,7},{7,0},{8,9},{9,10},{10,1... | collective-permute-start | bytes 98312 | tf_op jit(solution)/shard_map/while/body/eval_jaxpr/ppermute | solution.py:17
  102.3 15.6 %collective-permute-start.7 = (bf16[256,1024]{1,0:T(8,128)(2,1)S(1)}, bf16[256,1024]{1,0:T(8,128)(2,1)S(1)}, u32[]{:S(2)}, u32[]{:S(2)}) collective-permute-start(bf16[256,1024]{1,0:T(8,128)(2,1)S(1)} %get-tuple-element.467), channel_id=1, source_target_pairs={{0,8},{8,16},{16,24},{1,9},{9,17},{17,25},{2,10},{10,18},{18,26},{... | collective-permute-start | bytes 1572872 | tf_op jit(solution)/shard_map/while/body/eval_jaxpr/ppermute | solution.py:25
  119.8 12.3 %copy-start.1 = (s32[2,2,4]{2,1,0:T(2,128)S(1)}, s32[2,2,4]{2,1,0:T(2,128)}, u32[]{:S(2)}) copy-start(s32[2,2,4]{2,1,0:T(2,128)} %get-tuple-element.518) | copy-start | bytes 196 | tf_op jit(solution)/shard_map/while
  120.9 4.5 %collective-permute-start = (bf16[1,16,1024]{2,1,0:T(8,128)(2,1)S(1)}, bf16[1,16,1024]{2,1,0:T(8,128)(2,1)S(1)}, u32[]{:S(2)}, u32[]{:S(2)}) collective-permute-start(bf16[1,16,1024]{2,1,0:T(8,128)(2,1)S(1)} %get-tuple-element.459), channel_id=1, source_target_pairs={{0,7},{1,0},{2,1},{3,2},{4,3},{5,4},{6,5},{7,6},{8,15},{9,8},{10,9... | collective-permute-start | bytes 98312 | tf_op jit(solution)/shard_map/while/body/eval_jaxpr/ppermute | solution.py:17
  121.3 5.3 %collective-permute-start.1 = (bf16[1,16,1024]{2,1,0:T(8,128)(2,1)S(1)}, bf16[1,16,1024]{2,1,0:T(8,128)(2,1)S(1)}, u32[]{:S(2)}, u32[]{:S(2)}) collective-permute-start(bf16[1,16,1024]{2,1,0:T(8,128)(2,1)S(1)} %get-tuple-element.460), channel_id=1, source_target_pairs={{0,6},{1,7},{2,0},{3,1},{4,2},{5,3},{6,4},{7,5},{8,14},{9,15},{10,... | collective-permute-start | bytes 98312 | tf_op jit(solution)/shard_map/while/body/eval_jaxpr/ppermute | solution.py:17
  123.0 4.5 %collective-permute-start.2 = (bf16[1,16,1024]{2,1,0:T(8,128)(2,1)S(1)}, bf16[1,16,1024]{2,1,0:T(8,128)(2,1)S(1)}, u32[]{:S(2)}, u32[]{:S(2)}) collective-permute-start(bf16[1,16,1024]{2,1,0:T(8,128)(2,1)S(1)} %get-tuple-element.461), channel_id=1, source_target_pairs={{0,5},{1,6},{2,7},{3,0},{4,1},{5,2},{6,3},{7,4},{8,13},{9,14},{10,... | collective-permute-start | bytes 98312 | tf_op jit(solution)/shard_map/while/body/eval_jaxpr/ppermute | solution.py:17
  123.3 4.4 %collective-permute-start.3 = (bf16[1,16,1024]{2,1,0:T(8,128)(2,1)S(1)}, bf16[1,16,1024]{2,1,0:T(8,128)(2,1)S(1)}, u32[]{:S(2)}, u32[]{:S(2)}) collective-permute-start(bf16[1,16,1024]{2,1,0:T(8,128)(2,1)S(1)} %get-tuple-element.462), channel_id=1, source_target_pairs={{0,4},{1,5},{2,6},{3,7},{4,0},{5,1},{6,2},{7,3},{8,12},{9,13},{10,... | collective-permute-start | bytes 98312 | tf_op jit(solution)/shard_map/while/body/eval_jaxpr/ppermute | solution.py:17
  125.2 4.6 %collective-permute-start.4 = (bf16[1,16,1024]{2,1,0:T(8,128)(2,1)S(1)}, bf16[1,16,1024]{2,1,0:T(8,128)(2,1)S(1)}, u32[]{:S(2)}, u32[]{:S(2)}) collective-permute-start(bf16[1,16,1024]{2,1,0:T(8,128)(2,1)S(1)} %get-tuple-element.463), channel_id=1, source_target_pairs={{0,3},{1,4},{2,5},{3,6},{4,7},{5,0},{6,1},{7,2},{8,11},{9,12},{10,... | collective-permute-start | bytes 98312 | tf_op jit(solution)/shard_map/while/body/eval_jaxpr/ppermute | solution.py:17
  125.4 4.6 %collective-permute-start.5 = (bf16[1,16,1024]{2,1,0:T(8,128)(2,1)S(1)}, bf16[1,16,1024]{2,1,0:T(8,128)(2,1)S(1)}, u32[]{:S(2)}, u32[]{:S(2)}) collective-permute-start(bf16[1,16,1024]{2,1,0:T(8,128)(2,1)S(1)} %get-tuple-element.464), channel_id=1, source_target_pairs={{0,2},{1,3},{2,4},{3,5},{4,6},{5,7},{6,0},{7,1},{8,10},{9,11},{10,... | collective-permute-start | bytes 98312 | tf_op jit(solution)/shard_map/while/body/eval_jaxpr/ppermute | solution.py:17
  126.6 5.5 %collective-permute-start.6 = (bf16[1,16,1024]{2,1,0:T(8,128)(2,1)S(1)}, bf16[1,16,1024]{2,1,0:T(8,128)(2,1)S(1)}, u32[]{:S(2)}, u32[]{:S(2)}) collective-permute-start(bf16[1,16,1024]{2,1,0:T(8,128)(2,1)S(1)} %get-tuple-element.465), channel_id=1, source_target_pairs={{0,1},{1,2},{2,3},{3,4},{4,5},{5,6},{6,7},{7,0},{8,9},{9,10},{10,1... | collective-permute-start | bytes 98312 | tf_op jit(solution)/shard_map/while/body/eval_jaxpr/ppermute | solution.py:17
  132.2 13.3 %collective-permute-start.7 = (bf16[256,1024]{1,0:T(8,128)(2,1)S(1)}, bf16[256,1024]{1,0:T(8,128)(2,1)S(1)}, u32[]{:S(2)}, u32[]{:S(2)}) collective-permute-start(bf16[256,1024]{1,0:T(8,128)(2,1)S(1)} %get-tuple-element.467), channel_id=1, source_target_pairs={{0,8},{8,16},{16,24},{1,9},{9,17},{17,25},{2,10},{10,18},{18,26},{... | collective-permute-start | bytes 1572872 | tf_op jit(solution)/shard_map/while/body/eval_jaxpr/ppermute | solution.py:25
  145.6 1.0 copy-start
